TPU v7x, 256 devices: a whole 4x4x8 slice. The times are simulated.
256 devices in a mesh: pairs: 64 (over y, z, core), orb: 4 (over x).
Axes of the slice: x: 4, y: 4, z: 8, core: 2. Of those that a mesh axis runs over, the one named last changes fastest.
Arguments:
- amplitudes: float32 [1024, 128, 128], P(('pairs', 'orb')), may hold values from -4 to 4
- integrals: bfloat16 [1024, 128, 128], P(('pairs', 'orb')), may hold values from -6 to 6
- energies: float32 [1024, 128], P(('pairs', 'orb')), may hold values from 0.5 to 4
- intersections: bfloat16 [1024, 16, 128, 128], P(('pairs', 'orb')), may hold values from -0.5 to 0.5
- couplings: float32 [1024, 16], P(('pairs', 'orb')), may hold values from -2 to 2
- projector: float32 [1024, 128], P(('pairs', 'orb')), may hold values from -0.5 to 0.5
- pair_orbitals: int32 [1024, 2], P(('pairs', 'orb')), may hold values from 0 to 31
- coupled: int32 [1024, 16], replicated, may hold values from 0 to 1023, as said below
- pair_slot: int32 [1024], replicated, may hold values from 0 to 1023, as said below
Outputs:
- final_amplitudes: float32 [1024, 128, 128], P(('pairs', 'orb'))
- residual: float32 [1024, 128, 128], P(('pairs', 'orb'))
Inputs may be any that keep to these rules, and one draw needn't show every extreme that they name: `coupled`: each row holds 16 different pair ids, never the id of the pair held in that row's slot. The rows of one device name at most 1 different pairs held by the devices of any one pairs index, and exactly 1 held by the devices of the next pairs index. `pair_slot`: A permutation of the pair ids.
All inputs are finite; a program needn't handle non-finite values.
Results may differ from a plain program's by a relative error of at most 0.00037.
Values may be sent and summed in bfloat16 or wider, within the bound.
A program may use at most 64 MiB of HBM per device.

v0:
```python
import jax
import jax.numpy as jnp
from jax import lax
from jax.sharding import PartitionSpec as P

PAIRS_ORB = 32
ITERS = 2


def body(
    amplitudes,
    integrals,
    energies,
    intersections,
    couplings,
    projector,
    pair_orbitals,
    coupled,
    pair_slot,
):
    highest = lax.Precision.HIGHEST
    pair_count = lax.axis_size("pairs")
    orb_count = lax.axis_size("orb")
    devices = pair_count * orb_count
    per_device = amplitudes.shape[0]
    width = amplitudes.shape[1]
    total = coupled.shape[0]
    capacity = 1 + coupled.shape[1] // pair_count
    group = orb_count * per_device
    orbitals = total // PAIRS_ORB
    pair_idx = lax.axis_index("pairs")
    orb_idx = lax.axis_index("orb")
    device_id = pair_idx * orb_count + orb_idx
    targets = pair_slot[coupled]
    row_owner = jnp.broadcast_to(
        (jnp.arange(total, dtype=jnp.int32) // per_device)[:, None], targets.shape
    )
    needed = jnp.zeros((devices, total), jnp.int32).at[row_owner, targets].set(1)
    mine = lax.dynamic_slice_in_dim(needed, device_id, 1, 0)[0].reshape(pair_count, group)
    ranks = (jnp.cumsum(mine, axis=1) - 1).reshape(total)
    own_targets = lax.dynamic_slice_in_dim(targets, device_id * per_device, per_device, 0)
    slot_ids = jnp.arange(capacity, dtype=jnp.int32)
    group_cols = lax.dynamic_slice_in_dim(needed, pair_idx * group, group, 1)
    group_rank = jnp.cumsum(group_cols, axis=1) - 1
    entry_pos = own_targets // group * capacity + ranks[own_targets]
    dest_cols = group_cols.reshape(pair_count, orb_count, group)
    dest_cols = lax.dynamic_slice_in_dim(dest_cols, orb_idx, 1, 1)[:, 0]
    dest_rank = group_rank.reshape(pair_count, orb_count, group)
    dest_rank = lax.dynamic_slice_in_dim(dest_rank, orb_idx, 1, 1)[:, 0]
    select = (
        (dest_cols == 1)[:, None, :] & (dest_rank[:, None, :] == slot_ids[None, :, None])
    ).astype(jnp.bfloat16)
    orbital_ids = jnp.arange(orbitals, dtype=jnp.int32)
    first_hot = (pair_orbitals[:, 0:1] == orbital_ids[None, :]).astype(jnp.float32)
    second_hot = (pair_orbitals[:, 1:2] == orbital_ids[None, :]).astype(jnp.float32)
    denom = energies[:, :, None] + energies[:, None, :]
    state = amplitudes
    residual = amplitudes
    for step in range(ITERS):
        blocks = state.astype(jnp.bfloat16)
        group_blocks = lax.all_gather(blocks, "orb", axis=0, tiled=True)
        outgoing = jnp.einsum(
            "pcj,jxy->pcxy", select, group_blocks, preferred_element_type=jnp.float32
        )
        outgoing = outgoing.astype(jnp.bfloat16)
        arrived = lax.all_to_all(outgoing, "pairs", split_axis=0, concat_axis=0, tiled=True)
        arrived = arrived.reshape(pair_count * capacity, width, width)
        fetched = arrived[entry_pos]
        lifted = jnp.einsum(
            "pkab,pkbc->pkac", intersections, fetched, preferred_element_type=jnp.float32
        )
        scaled = (couplings[:, :, None, None] * lifted).astype(jnp.bfloat16)
        coupling = jnp.einsum(
            "pkac,pkdc->pad", scaled, intersections, preferred_element_type=jnp.float32
        )
        projected = jnp.einsum("pab,pb->pa", state, projector, precision=highest)
        partial_sum = jnp.dot(first_hot.T, projected, precision=highest) + jnp.dot(
            second_hot.T, projected, precision=highest
        )
        summed = lax.psum(partial_sum, ("pairs", "orb"))
        left = jnp.dot(first_hot, summed, precision=highest)
        right = jnp.dot(second_hot, summed, precision=highest)
        residual = (
            integrals.astype(jnp.float32)
            + energies[:, :, None] * state
            + state * energies[:, None, :]
            - coupling
            + left[:, :, None] * projector[:, None, :]
            + projector[:, :, None] * right[:, None, :]
        )
        state = state - residual / denom
    return (state, residual)


def solution(mesh):
    return jax.shard_map(
        body,
        mesh=mesh,
        in_specs=(
            P(("pairs", "orb"), None, None),
            P(("pairs", "orb"), None, None),
            P(("pairs", "orb"), None),
            P(("pairs", "orb"), None, None, None),
            P(("pairs", "orb"), None),
            P(("pairs", "orb"), None),
            P(("pairs", "orb"), None),
            P(),
            P(),
        ),
        out_specs=(P(("pairs", "orb"), None, None), P(("pairs", "orb"), None, None)),
        check_vma=False,
    )
```

profile of v0, /device:TPU:1, one launch (start us, length us, event | category | flops | bytes accessed | tf_op | source)
XLA Modules:
  0.0 392.0 jit_solution(17940552267861765877)
XLA Ops:
  0.7 0.6 add_select_fusion
  1.3 0.6 broadcast_compare_fusion
  1.9 0.8 compare_select_fusion.1
  3.1 65.3 %gather_fusion = s32[16384]{0:T(1024)S(1)} fusion(s32[1024]{0:T(1024)S(1)} %copy-done.1, s32[16384]{0:T(1024)S(1)} %broadcast_clamp_fusion), kind=kCustom, calls=%fused_computation | custom fusion | bytes 196608 | tf_op jit(solution)/shard_map/gather | solution.py:34
  68.9 0.2 copy-done.3
  69.8 0.6 broadcast.186
  70.4 60.8 %scatter_custom_fusion = s32[262144]{0:T(1024)S(1)} fusion(s32[16384]{0:T(1024)S(1)} %reshape.167, s32[16384]{0:T(1024)} %broadcast.186, s32[]{:T(128)} %constant.52.clone.1), kind=kCustom, calls=%fused_computation.28 | custom fusion | bytes 1049088
  131.2 1.1 reshape.134
  132.3 1.0 constant_dynamic-slice_fusion
  133.4 0.7 reduce_window_sum.22
  134.1 12.3 %all_gather.6 = bf16[16,128,128]{2,1,0:T(8,128)(2,1)S(1)} all-gather(bf16[4,128,128]{2,1,0:T(8,128)(2,1)S(1)} %convert_element_type.38), channel_id=1, replica_groups=mesh['pairs'=64,'orb'=4] {'orb'}, dimensions={0}, use_global_device_ids=true | all-gather | bytes 655360 | tf_op jit(solution)/shard_map/all_gather | solution.py:61
  146.4 0.7 convert_bitcast_fusion.1
  147.1 2.6 copy.45
  149.8 14.2 %all-to-all-start = ((bf16[64,1,128,128]{3,2,1,0:T(8,128)(2,1)}), bf16[64,1,128,128]{3,2,1,0:T(8,128)(2,1)}, u32[]{:S(2)}, u32[]{:S(2)}) async-start(bf16[64,1,128,128]{3,2,1,0:T(8,128)(2,1)} %copy.45), calls=%async_computation | async-start | bytes 4194304 | tf_op jit(solution)/shard_map/all_to_all | solution.py:66
  164.2 0.8 dynamic-slice_reduce_fusion
  165.4 0.7 gather_fusion.1
  166.4 0.5 fusion.65
  166.9 0.3 fusion.54
  167.2 0.3 convolution_add_fusion.1
  167.4 89.2 %psum.14 = f32[32,128]{1,0:T(8,128)S(1)} all-reduce(f32[32,128]{1,0:T(8,128)S(1)} %convolution_add_fusion.1), channel_id=1, replica_groups=mesh['pairs'=64,'orb'=4] {'pairs','orb'}, use_global_device_ids=true, to_apply=%region_3.4 | all-reduce | flops 4096 | bytes 32768 | tf_op jit(solution)/shard_map/psum | solution.py:80
  257.1 3.7 gather_fusion.2
  260.8 3.8 fusion.64
  264.6 11.4 %all_gather.7 = bf16[16,128,128]{2,1,0:T(8,128)(2,1)S(1)} all-gather(bf16[4,128,128]{2,1,0:T(8,128)(2,1)S(1)} %get-tuple-element.4), channel_id=1, replica_groups=mesh['pairs'=64,'orb'=4] {'orb'}, dimensions={0}, use_global_device_ids=true | all-gather | bytes 655360 | tf_op jit(solution)/shard_map/all_gather | solution.py:61
  276.1 0.7 convert_bitcast_fusion
  276.8 2.6 copy.50
  279.4 11.7 %all-to-all-start.1 = ((bf16[64,1,128,128]{3,2,1,0:T(8,128)(2,1)}), bf16[64,1,128,128]{3,2,1,0:T(8,128)(2,1)}, u32[]{:S(2)}, u32[]{:S(2)}) async-start(bf16[64,1,128,128]{3,2,1,0:T(8,128)(2,1)} %copy.50), calls=%async_computation.1 | async-start | bytes 4194304 | tf_op jit(solution)/shard_map/all_to_all | solution.py:66
  291.1 0.5 fusion.66
  291.6 0.3 fusion.52
  291.9 0.3 convolution_add_fusion
  292.2 91.1 %psum.15 = f32[32,128]{1,0:T(8,128)S(1)} all-reduce(f32[32,128]{1,0:T(8,128)S(1)} %convolution_add_fusion), channel_id=1, replica_groups=mesh['pairs'=64,'orb'=4] {'pairs','orb'}, use_global_device_ids=true, to_apply=%region_4.5 | all-reduce | flops 4096 | bytes 32768 | tf_op jit(solution)/shard_map/psum | solution.py:80
  383.7 3.7 gather_fusion.3
  387.4 4.6 %fusion.40 = (f32[4,128,128]{2,1,0:T(8,128)}, f32[4,128,128]{2,1,0:T(8,128)}) fusion(f32[4,128,128]{2,1,0:T(8,128)S(1)} %get-tuple-element.5, f32[4,128]{1,0:T(4,128)S(1)} %copy-done.12, f32[4,128]{1,0:T(4,128)S(1)} %fusion.49, f32[4,128]{1,0:T(4,128)S(1)} %copy-done.5, f32[4,128]{1,0:T(4,128)S(1)} %fusion.51, bf16[4,16,128,128]{3,2,1,0:T(8,128)(2,1)S(1)} %copy-done, ...), kind=kOutput, calls=%fused_computation.35 | convolution fusion | flops 539820032 | bytes 5120256 | tf_op jit(solution)/shard_map/pkac,pkdc->pad/dot_general | solution.py:73
  (59 shorter events, 3.1 us)
Async XLA Ops:
  0.6 260.2 %copy-start = (bf16[4,16,128,128]{3,2,1,0:T(8,128)(2,1)S(1)}, bf16[4,16,128,128]{3,2,1,0:T(8,128)(2,1)}, u32[]{:S(2)}) copy-start(bf16[4,16,128,128]{3,2,1,0:T(8,128)(2,1)} %param.12) | copy-start | bytes 6291460
  0.6 2.5 copy-start.1
  68.4 0.7 copy-start.3
  68.4 0.7 copy-start.4
  68.4 0.7 copy-start.6
  68.4 0.7 copy-start.9
  68.4 0.8 copy-start.8
  69.7 64.4 %copy-start.2 = (f32[4,128,128]{2,1,0:T(8,128)S(1)}, f32[4,128,128]{2,1,0:T(8,128)}, u32[]{:S(2)}) copy-start(f32[4,128,128]{2,1,0:T(8,128)} %param.9) | copy-start | bytes 786436
  149.8 107.3 %all-to-all-start = ((bf16[64,1,128,128]{3,2,1,0:T(8,128)(2,1)}), bf16[64,1,128,128]{3,2,1,0:T(8,128)(2,1)}, u32[]{:S(2)}, u32[]{:S(2)}) async-start(bf16[64,1,128,128]{3,2,1,0:T(8,128)(2,1)} %copy.45), calls=%async_computation | async-start | bytes 4194304 | tf_op jit(solution)/shard_map/all_to_all | solution.py:66
  164.0 2.4 copy-start.7
  164.0 2.4 copy-start.5
  257.0 3.8 copy-start.10
  257.0 3.8 copy-start.11
  257.1 3.8 copy-start.12
  279.4 104.3 %all-to-all-start.1 = ((bf16[64,1,128,128]{3,2,1,0:T(8,128)(2,1)}), bf16[64,1,128,128]{3,2,1,0:T(8,128)(2,1)}, u32[]{:S(2)}, u32[]{:S(2)}) async-start(bf16[64,1,128,128]{3,2,1,0:T(8,128)(2,1)} %copy.50), calls=%async_computation.1 | async-start | bytes 4194304 | tf_op jit(solution)/shard_map/all_to_all | solution.py:66
where the time goes:
time: 393 us; the launch traced here: 392 us
  blocking collectives  204 us (52%)
  local copies, waits for them, and re-layouts  145 us (37%)
  starting transfers between devices  25.9 us (7%)
  matrix products  12.6 us (3%)
    psum x2, blocking collectives, body(): summed = lax.psum(partial_sum, ('pairs', 'orb'))  180 us
    gather x3, local copies, waits for them, and re-layouts, body(): targets = pair_slot[coupled]  65.6 us
    unnamed x30, local copies, waits for them, and re-layouts  62.1 us
    all_to_all x2, starting transfers between devices, body(): lax.all_to_all(outgoing, 'pairs', split_axis=0, concat_axis=0, tiled=True)  25.9 us
    all_gather x2, blocking collectives, body(): group_blocks = lax.all_gather(blocks, 'orb', axis=0, tiled=True)  23.7 us
    dot_general x2, matrix products, body(): jnp.einsum('pkac,pkdc->pad', scaled, intersections, preferred_element_typ...  8.38 us
  transfers between devices with their start and end apart: 2, of which 0 were waited for; matrix products, arithmetic and copies ran while one was open for 1% of the time, Pallas kernels for 0%

commit v1 on v0

--- a/solution.py
+++ b/solution.py
@@ -5,6 +5,24 @@
 
 PAIRS_ORB = 32
 ITERS = 2
+
+
+def ring_gather(array, axis, dim):
+    ways, here, step = (lax.axis_size(axis), lax.axis_index(axis), array.shape[dim])
+    shape = [n * ways if d == dim else n for d, n in enumerate(array.shape)]
+    full = lax.dynamic_update_slice_in_dim(
+        jnp.zeros(shape, array.dtype), array, here * step, axis=dim
+    )
+    going_up = going_down = array
+    for far in range(1, ways // 2 + 1):
+        going_up = lax.ppermute(going_up, axis, [(d, (d + 1) % ways) for d in range(ways)])
+        full = lax.dynamic_update_slice_in_dim(full, going_up, (here - far) % ways * step, axis=dim)
+        if 2 * far < ways:
+            going_down = lax.ppermute(going_down, axis, [(d, (d - 1) % ways) for d in range(ways)])
+            full = lax.dynamic_update_slice_in_dim(
+                full, going_down, (here + far) % ways * step, axis=dim
+            )
+    return full
 
 
 def body(
@@ -58,7 +76,7 @@
     residual = amplitudes
     for step in range(ITERS):
         blocks = state.astype(jnp.bfloat16)
-        group_blocks = lax.all_gather(blocks, "orb", axis=0, tiled=True)
+        group_blocks = ring_gather(blocks, "orb", 0)
         outgoing = jnp.einsum(
             "pcj,jxy->pcxy", select, group_blocks, preferred_element_type=jnp.float32
         )

time: 393 us -> 390 us (level)
  blocking collectives: 204 us -> 180 us
  waiting for transfers between devices: 0.01 us -> 12.4 us
    all_gather x2 -> x0, blocking collectives: 23.7 us -> none  [body(): group_blocks = lax.all_gather(blocks, 'orb', axis=0, tiled=True)]
    ppermute x0 -> x6, waiting for transfers between devices: none -> 12.4 us  [the longest x4 12.4 us: ring_gather(): lax.ppermute(going_up, axis, [(d, (d + 1) % ways) for d in range(ways)])]
    ppermute x0 -> x6, starting transfers between devices: none -> 5.38 us  [the longest x2 5.1 us: ring_gather(): lax.ppermute(going_down, axis, [(d, (d - 1) % ways) for d in range(ways)])]
    dynamic_update_slice x0 -> x8, local copies, waits for them, and re-layouts: none -> 3.94 us  [the longest x4 1.52 us: ring_gather(): lax.dynamic_update_slice_in_dim(full, going_up, (here - far) % ways * ste...]
  transfers between devices with their start and end apart: 2 -> 8, of which waited for: 0 -> 3; matrix products, arithmetic and copies ran while one was open for 1% -> 36% of each run, Pallas kernels for 0% -> 0%
where the time goes in v1:
time: 390 us; the launch traced here: 389 us
  blocking collectives  180 us (46%)
  local copies, waits for them, and re-layouts  148 us (38%)
  starting transfers between devices  29.6 us (8%)
  matrix products  12.6 us (3%)
  waiting for transfers between devices  12.4 us (3%)
  other arithmetic  5.07 us (1%)
    psum x2, blocking collectives, body(): summed = lax.psum(partial_sum, ('pairs', 'orb'))  180 us
    gather x3, local copies, waits for them, and re-layouts, body(): targets = pair_slot[coupled]  65.6 us
    unnamed x30, local copies, waits for them, and re-layouts  61.3 us
    all_to_all x2, starting transfers between devices, body(): lax.all_to_all(outgoing, 'pairs', split_axis=0, concat_axis=0, tiled=True)  24.2 us
    ppermute x4, waiting for transfers between devices, ring_gather(): lax.ppermute(going_up, axis, [(d, (d + 1) % ways) for d in range(ways)])  12.4 us
    dot_general x2, matrix products, body(): jnp.einsum('pkac,pkdc->pad', scaled, intersections, preferred_element_typ...  8.38 us
  transfers between devices with their start and end apart: 8, of which 3 were waited for; matrix products, arithmetic and copies ran while one was open for 36% of the time, Pallas kernels for 0%

profile of v1, /device:TPU:1, one launch (start us, length us, event | category | flops | bytes accessed | tf_op | source)
XLA Modules:
  0.0 389.0 jit_solution(9888384662249228349)
XLA Ops:
  0.7 1.8 convert_element_type.38
  2.4 3.3 collective-permute-start.1
  5.7 0.6 broadcast_compare_fusion
  6.3 0.6 add_select_fusion
  6.9 0.8 compare_select_fusion.1
  8.2 65.3 %gather_fusion = s32[16384]{0:T(1024)S(1)} fusion(s32[1024]{0:T(1024)S(1)} %copy-done.1, s32[16384]{0:T(1024)S(1)} %broadcast_clamp_fusion), kind=kCustom, calls=%fused_computation | custom fusion | bytes 196608 | tf_op jit(solution)/shard_map/gather | solution.py:52
  74.8 60.6 %scatter_custom_fusion = s32[262144]{0:T(1024)S(1)} fusion(s32[16384]{0:T(1024)S(1)} %reshape.167, s32[16384]{0:T(1024)S(1)} %broadcast.193, s32[]{:T(128)} %constant.80.clone.1), kind=kCustom, calls=%fused_computation.26 | custom fusion | bytes 1048580
  135.4 1.1 reshape.134
  136.6 1.1 copy_dynamic-update-slice_fusion.7
  137.7 1.0 constant_dynamic-slice_fusion.1
  138.8 0.7 reduce_window_sum.22
  139.8 1.1 copy_dynamic-update-slice_fusion.6
  140.9 1.1 copy_dynamic-update-slice_fusion.5
  142.0 2.9 collective-permute-done.2
  145.0 0.7 convert_bitcast_fusion.1
  145.7 2.7 copy.66
  148.4 13.9 %all-to-all-start = ((bf16[64,1,128,128]{3,2,1,0:T(8,128)(2,1)}), bf16[64,1,128,128]{3,2,1,0:T(8,128)(2,1)}, u32[]{:S(2)}, u32[]{:S(2)}) async-start(bf16[64,1,128,128]{3,2,1,0:T(8,128)(2,1)} %copy.66), calls=%async_computation | async-start | bytes 4194304 | tf_op jit(solution)/shard_map/all_to_all | solution.py:84
  162.7 0.8 dynamic-slice_reduce_fusion
  163.8 0.7 gather_fusion.1
  165.8 88.7 %psum.14 = f32[32,128]{1,0:T(8,128)S(1)} all-reduce(f32[32,128]{1,0:T(8,128)S(1)} %convolution_add_fusion.1), channel_id=1, replica_groups=mesh['pairs'=64,'orb'=4] {'pairs','orb'}, use_global_device_ids=true, to_apply=%region_3.4 | all-reduce | flops 4096 | bytes 32768 | tf_op jit(solution)/shard_map/psum | solution.py:98
  254.9 3.8 gather_fusion.2
  258.7 3.8 fusion.62
  262.5 1.8 collective-permute-start.4
  264.6 4.8 %collective-permute-done.3 = bf16[4,128,128]{2,1,0:T(8,128)(2,1)S(1)} collective-permute-done((bf16[4,128,128]{2,1,0:T(8,128)(2,1)S(1)}, bf16[4,128,128]{2,1,0:T(8,128)(2,1)S(1)}, u32[]{:S(2)}, u32[]{:S(2)}) %collective-permute-start.3) | collective-permute-done | bytes 131104 | tf_op jit(solution)/shard_map/ppermute | solution.py:18
  269.7 4.7 %collective-permute-done.5 = bf16[4,128,128]{2,1,0:T(8,128)(2,1)S(1)} collective-permute-done((bf16[4,128,128]{2,1,0:T(8,128)(2,1)S(1)}, bf16[4,128,128]{2,1,0:T(8,128)(2,1)S(1)}, u32[]{:S(2)}, u32[]{:S(2)}) %collective-permute-start.5) | collective-permute-done | bytes 131104 | tf_op jit(solution)/shard_map/ppermute | solution.py:18
  274.5 0.7 convert_bitcast_fusion
  275.2 2.7 copy.74
  277.9 10.3 %all-to-all-start.1 = ((bf16[64,1,128,128]{3,2,1,0:T(8,128)(2,1)}), bf16[64,1,128,128]{3,2,1,0:T(8,128)(2,1)}, u32[]{:S(2)}, u32[]{:S(2)}) async-start(bf16[64,1,128,128]{3,2,1,0:T(8,128)(2,1)} %copy.74), calls=%async_computation.1 | async-start | bytes 4194304 | tf_op jit(solution)/shard_map/all_to_all | solution.py:84
  288.2 0.5 fusion.64
  289.2 91.1 %psum.15 = f32[32,128]{1,0:T(8,128)S(1)} all-reduce(f32[32,128]{1,0:T(8,128)S(1)} %convolution_add_fusion), channel_id=1, replica_groups=mesh['pairs'=64,'orb'=4] {'pairs','orb'}, use_global_device_ids=true, to_apply=%region_4.5 | all-reduce | flops 4096 | bytes 32768 | tf_op jit(solution)/shard_map/psum | solution.py:98
  380.7 3.7 gather_fusion.3
  384.5 4.6 %fusion.38 = (f32[4,128,128]{2,1,0:T(8,128)}, f32[4,128,128]{2,1,0:T(8,128)}) fusion(f32[4,128,128]{2,1,0:T(8,128)S(1)} %get-tuple-element.5, f32[4,128]{1,0:T(4,128)S(1)} %copy-done.12, f32[4,128]{1,0:T(4,128)S(1)} %fusion.47, f32[4,128]{1,0:T(4,128)S(1)} %copy-done.5, f32[4,128]{1,0:T(4,128)S(1)} %fusion.49, bf16[4,16,128,128]{3,2,1,0:T(8,128)(2,1)S(1)} %copy-done, ...), kind=kOutput, calls=%fused_computation.33 | convolution fusion | flops 539820032 | bytes 5120256 | tf_op jit(solution)/shard_map/pkac,pkdc->pad/dot_general | solution.py:91
  (79 shorter events, 6.1 us)
Async XLA Ops:
  0.6 258.1 %copy-start = (bf16[4,16,128,128]{3,2,1,0:T(8,128)(2,1)S(1)}, bf16[4,16,128,128]{3,2,1,0:T(8,128)(2,1)}, u32[]{:S(2)}) copy-start(bf16[4,16,128,128]{3,2,1,0:T(8,128)(2,1)} %param.12) | copy-start | bytes 6291460
  0.6 7.5 %copy-start.1 = (s32[1024]{0:T(1024)S(1)}, s32[1024]{0:T(1024)}, u32[]{:S(2)}) copy-start(s32[1024]{0:T(1024)} %param.17) | copy-start | bytes 12292
  2.4 138.5 %collective-permute-start.1 = (bf16[4,128,128]{2,1,0:T(8,128)(2,1)}, bf16[4,128,128]{2,1,0:T(8,128)(2,1)}, u32[]{:S(2)}, u32[]{:S(2)}) collective-permute-start(bf16[4,128,128]{2,1,0:T(8,128)(2,1)} %convert_element_type.38), channel_id=1, source_target_pairs={{0,3},{1,0},{2,1},{3,2},{4,7},{5,4},{6,5},{7,6},{8,11},{9,8},{10,9... | collective-permute-start | bytes 393224 | tf_op jit(solution)/shard_map/ppermute | solution.py:21
  5.7 133.8 %collective-permute-start = (bf16[4,128,128]{2,1,0:T(8,128)(2,1)}, bf16[4,128,128]{2,1,0:T(8,128)(2,1)}, u32[]{:S(2)}, u32[]{:S(2)}) collective-permute-start(bf16[4,128,128]{2,1,0:T(8,128)(2,1)} %convert_element_type.38), channel_id=1, source_target_pairs={{0,1},{1,2},{2,3},{3,0},{4,5},{5,6},{6,7},{7,4},{8,9},{9,10},{10,1... | collective-permute-start | bytes 393224 | tf_op jit(solution)/shard_map/ppermute | solution.py:18
  73.5 0.7 copy-start.3
  73.5 0.7 copy-start.4
  73.5 0.7 copy-start.6
  73.5 0.7 copy-start.9
  73.5 0.8 copy-start.8
  139.6 5.3 %collective-permute-start.2 = (bf16[4,128,128]{2,1,0:T(8,128)(2,1)}, bf16[4,128,128]{2,1,0:T(8,128)(2,1)S(1)}, u32[]{:S(2)}, u32[]{:S(2)}) collective-permute-start(bf16[4,128,128]{2,1,0:T(8,128)(2,1)} %collective-permute-done), channel_id=1, source_target_pairs={{0,1},{1,2},{2,3},{3,0},{4,5},{5,6},{6,7},{7,4},{8,9},{9,10},{10,1... | collective-permute-start | bytes 393224 | tf_op jit(solution)/shard_map/ppermute | solution.py:18
  148.4 106.5 %all-to-all-start = ((bf16[64,1,128,128]{3,2,1,0:T(8,128)(2,1)}), bf16[64,1,128,128]{3,2,1,0:T(8,128)(2,1)}, u32[]{:S(2)}, u32[]{:S(2)}) async-start(bf16[64,1,128,128]{3,2,1,0:T(8,128)(2,1)} %copy.66), calls=%async_computation | async-start | bytes 4194304 | tf_op jit(solution)/shard_map/all_to_all | solution.py:84
  162.3 2.4 copy-start.7
  162.3 2.4 copy-start.2
  162.4 2.4 copy-start.5
  254.9 3.8 copy-start.10
  254.9 3.8 copy-start.11
  254.9 3.8 copy-start.12
  262.5 7.0 %collective-permute-start.4 = (bf16[4,128,128]{2,1,0:T(8,128)(2,1)S(1)}, bf16[4,128,128]{2,1,0:T(8,128)(2,1)S(1)}, u32[]{:S(2)}, u32[]{:S(2)}) collective-permute-start(bf16[4,128,128]{2,1,0:T(8,128)(2,1)S(1)} %get-tuple-element.4), channel_id=1, source_target_pairs={{0,3},{1,0},{2,1},{3,2},{4,7},{5,4},{6,5},{7,6},{8,11},{9,8},{10,9... | collective-permute-start | bytes 393224 | tf_op jit(solution)/shard_map/ppermute | solution.py:21
  264.3 5.0 %collective-permute-start.3 = (bf16[4,128,128]{2,1,0:T(8,128)(2,1)S(1)}, bf16[4,128,128]{2,1,0:T(8,128)(2,1)S(1)}, u32[]{:S(2)}, u32[]{:S(2)}) collective-permute-start(bf16[4,128,128]{2,1,0:T(8,128)(2,1)S(1)} %get-tuple-element.4), channel_id=1, source_target_pairs={{0,1},{1,2},{2,3},{3,0},{4,5},{5,6},{6,7},{7,4},{8,9},{9,10},{10,1... | collective-permute-start | bytes 393224 | tf_op jit(solution)/shard_map/ppermute | solution.py:18
  269.4 5.0 %collective-permute-start.5 = (bf16[4,128,128]{2,1,0:T(8,128)(2,1)S(1)}, bf16[4,128,128]{2,1,0:T(8,128)(2,1)S(1)}, u32[]{:S(2)}, u32[]{:S(2)}) collective-permute-start(bf16[4,128,128]{2,1,0:T(8,128)(2,1)S(1)} %collective-permute-done.3), channel_id=1, source_target_pairs={{0,1},{1,2},{2,3},{3,0},{4,5},{5,6},{6,7},{7,4},{8,9},{9,10},{10,1... | collective-permute-start | bytes 393224 | tf_op jit(solution)/shard_map/ppermute | solution.py:18
  277.9 102.8 %all-to-all-start.1 = ((bf16[64,1,128,128]{3,2,1,0:T(8,128)(2,1)}), bf16[64,1,128,128]{3,2,1,0:T(8,128)(2,1)}, u32[]{:S(2)}, u32[]{:S(2)}) async-start(bf16[64,1,128,128]{3,2,1,0:T(8,128)(2,1)} %copy.74), calls=%async_computation.1 | async-start | bytes 4194304 | tf_op jit(solution)/shard_map/all_to_all | solution.py:84
